TPU v7x, 128 devices: a whole 4x4x4 slice. The times are simulated.
128 devices in a mesh: grid: 32 (over y_lo, x, z), ch: 4 (over y_hi, core).
Axes of the slice: x: 4, y: 4 (y_hi: 2, y_lo: 2; y = y_hi * 2 + y_lo), z: 4, core: 2. Of those that a mesh axis runs over, the one named last changes fastest.
Arguments:
- inputs: bfloat16 [128, 1024, 512], P('grid', None, 'ch'), may hold values from -6 to 6
- w_gate: bfloat16 [512, 512], P(None, 'ch'), may hold values from -0.25 to 0.25
- w_value: bfloat16 [512, 512], P(None, 'ch'), may hold values from -0.25 to 0.25
- short_filter: bfloat16 [2, 3, 3, 512], P(None, None, None, 'ch'), may hold values from -2 to 2
- row_filter: bfloat16 [1024, 512], P(None, 'ch'), may hold values from -0.1875 to 0.1875
- column_filter: bfloat16 [128, 512], P(None, 'ch'), may hold values from -0.5 to 0.5
- cotangent: bfloat16 [128, 1024, 512], P('grid', None, 'ch'), may hold values from -6 to 6
Outputs:
- gated: bfloat16 [128, 1024, 512], P('grid', None, 'ch')
- input_grad: bfloat16 [128, 1024, 512], P('grid', None, 'ch')
- gate_grad: float32 [512, 512], P('grid', 'ch')
- value_grad: float32 [512, 512], P('grid', 'ch')
- short_grad: float32 [2, 3, 3, 512], P(None, None, None, 'ch')
- row_grad: float32 [1024, 512], P('grid', 'ch')
- column_grad: float32 [128, 512], P('grid', 'ch')
All inputs are finite; a program needn't handle non-finite values.
Results may differ from a plain program's by a relative error of at most 0.025.
Values may be sent and summed in bfloat16 or wider, within the bound.
No kernel may reach another device: no remote copies, remote signals or barrier semaphores. Data moves between devices by JAX's collectives and lax.ppermute only.
A program may use at most 128 MiB of HBM per device.

v0:
```python
import math
import jax
import jax.numpy as jnp
from jax import lax
from jax.sharding import PartitionSpec as P

highest = lax.Precision.HIGHEST


def extended(value, sides, width):
    for axis, dim in sides:
        size, length = (lax.axis_size(axis), value.shape[dim])
        up = [(i, (i + 1) % size) for i in range(size - 1)]
        down = [(j, i) for i, j in up]
        last = lax.slice_in_dim(value, length - width, length, axis=dim)
        initial = lax.slice_in_dim(value, 0, width, axis=dim)
        before = lax.ppermute(last, axis, up)
        after = lax.ppermute(initial, axis, down)
        value = jnp.concatenate([before, value, after], axis=dim)
    return value


def sent_to_all(value, axis):
    copies = jnp.broadcast_to(value, (lax.axis_size(axis), *value.shape))
    return lax.all_to_all(copies, axis, split_axis=0, concat_axis=0, tiled=True)


def taken_together(value, axis):
    return sent_to_all(value, axis).sum(axis=0)


def in_one_piece(arrays, axis, dim, along):
    both = jnp.concatenate(arrays, axis=along)
    out, at, finished = (lax.psum_scatter(both, axis, scatter_dimension=dim, tiled=True), 0, [])
    for a in arrays:
        finished.append(lax.slice_in_dim(out, at, at + a.shape[along], axis=along))
        at += a.shape[along]
    return tuple(finished)


def hartley(length):
    position = jnp.arange(length, dtype=jnp.int32)
    product = position[:, None] * position[None, :] % length
    phases = product.astype(jnp.float32) * (2.0 * math.pi / length)
    return jnp.cos(phases) + jnp.sin(phases)


def mirror(values, along):
    leading = lax.slice_in_dim(values, 0, 1, axis=along)
    remainder = lax.slice_in_dim(values, 1, values.shape[along], axis=along)
    return jnp.concatenate([leading, jnp.flip(remainder, along)], axis=along)


def even_odd(spectrum, along):
    reversed_spec = mirror(spectrum, along)
    return (0.5 * (spectrum + reversed_spec), 0.5 * (spectrum - reversed_spec))


def column_forward(row_cols, cas_height, col_even, col_odd):
    spec_rows = jnp.einsum("hwc,hk->kwc", row_cols, cas_height, precision=highest)
    second = spec_rows * col_even[:, None] + mirror(spec_rows, 0) * col_odd[:, None]
    mixed_cols = (
        jnp.einsum("kwc,kh->hwc", second, cas_height, precision=highest) / cas_height.shape[0]
    )
    return (spec_rows, mixed_cols)


def column_backward(grad_cols, spec_rows, cas_height, col_even, col_odd, scale):
    full_height = cas_height.shape[0]
    spec_grad = jnp.einsum("hwc,hk->kwc", grad_cols, cas_height, precision=highest)
    mirrored_grad = mirror(spec_grad, 0)
    back_cols = spec_grad * col_even[:, None] - mirrored_grad * col_odd[:, None]
    grad_row_cols = (
        jnp.einsum("kwc,kh->hwc", back_cols, cas_height, precision=highest) / full_height
    )
    rows_even, rows_odd = even_odd(spec_rows, 0)
    col_term = jnp.sum(spec_grad * rows_even - mirrored_grad * rows_odd, axis=1)
    col_grad = jnp.einsum("kc,km->mc", col_term, cas_height, precision=highest) * (
        scale / full_height
    )
    return (grad_row_cols, col_grad)


def local(inputs, w_gate, w_value, short_filter, row_filter, column_filter, cotangent):
    tile_rows, full_width, channels = inputs.shape
    gathered = lax.all_gather(inputs, "ch", axis=2, tiled=True)
    w_both = jnp.concatenate([w_gate, w_value], axis=1)
    stacked = jnp.einsum(
        "rwd,dc->rwc", gathered, w_both, preferred_element_type=jnp.float32
    ).astype(jnp.bfloat16)
    kernel = jnp.concatenate([short_filter[0], short_filter[1]], axis=-1).astype(jnp.float32)
    framed = extended(stacked, (("grid", 0),), 1)
    framed = jnp.pad(framed, ((0, 0), (1, 1), (0, 0))).astype(jnp.float32)
    featured = jnp.zeros((tile_rows, full_width, 2 * channels), jnp.float32)
    for row_shift in range(3):
        for col_shift in range(3):
            featured = (
                featured
                + kernel[row_shift, col_shift]
                * framed[row_shift : row_shift + tile_rows, col_shift : col_shift + full_width]
            )
    featured = featured.astype(jnp.bfloat16)
    gate_feat = featured[..., :channels].astype(jnp.float32)
    value_bf = featured[..., channels:]
    cas_width = hartley(full_width)
    width_high = cas_width.astype(jnp.bfloat16)
    width_low = (cas_width - width_high.astype(jnp.float32)).astype(jnp.bfloat16)
    spec_b = jnp.einsum("rwc,wk->rkc", value_bf, width_high, preferred_element_type=jnp.float32)
    spec_b = spec_b + jnp.einsum(
        "rwc,wk->rkc", value_bf, width_low, preferred_element_type=jnp.float32
    )
    row_spec = jnp.einsum("mc,mk->kc", row_filter.astype(jnp.float32), cas_width, precision=highest)
    row_even, row_odd = even_odd(row_spec, 0)
    row_mixed = spec_b * row_even + mirror(spec_b, 1) * row_odd
    mix_row = jnp.einsum("rkc,kw->rwc", row_mixed, cas_width, precision=highest) / full_width
    full_height = column_filter.shape[0]
    cas_height = hartley(full_height)
    col_spec = jnp.einsum(
        "mc,mk->kc", column_filter.astype(jnp.float32), cas_height, precision=highest
    )
    col_even, col_odd = even_odd(col_spec, 0)
    scale = 1.0 / math.sqrt(full_height * full_width)
    grad_out = cotangent.astype(jnp.float32)
    grad_mix = grad_out * gate_feat
    row_cols = lax.all_to_all(mix_row, "grid", split_axis=1, concat_axis=0, tiled=True)
    spec_rows, mixed_cols = column_forward(row_cols, cas_height, col_even, col_odd)
    mix_col = lax.all_to_all(mixed_cols, "grid", split_axis=0, concat_axis=1, tiled=True)
    grad_cols = lax.all_to_all(grad_mix, "grid", split_axis=1, concat_axis=0, tiled=True)
    grad_row_cols, col_grad = column_backward(
        grad_cols, spec_rows, cas_height, col_even, col_odd, scale
    )
    grad_row = lax.all_to_all(grad_row_cols, "grid", split_axis=0, concat_axis=1, tiled=True)
    gated = (gate_feat * mix_col).astype(jnp.bfloat16)
    grad_gate = grad_out * mix_col
    spec_gr = jnp.einsum("rwc,wk->rkc", grad_row, cas_width, precision=highest)
    mirrored_gr = mirror(spec_gr, 1)
    back_rows = spec_gr * row_even - mirrored_gr * row_odd
    grad_value = jnp.einsum("rkc,kw->rwc", back_rows, cas_width, precision=highest) / full_width
    value_even, value_odd = even_odd(spec_b, 1)
    row_term = jnp.sum(spec_gr * value_even - mirrored_gr * value_odd, axis=0)
    row_grad = jnp.einsum("kc,km->mc", row_term, cas_width, precision=highest) * (
        scale / full_width
    )
    grad_feat = jnp.concatenate([grad_gate, grad_value], axis=2)
    grad_framed = extended(grad_feat, (("grid", 0),), 1)
    grad_framed = jnp.pad(grad_framed, ((0, 0), (1, 1), (0, 0)))
    back_sum = jnp.zeros((tile_rows, full_width, 2 * channels), jnp.float32)
    short_rows = []
    for row_shift in range(3):
        short_cols = []
        for col_shift in range(3):
            back_sum = (
                back_sum
                + kernel[row_shift, col_shift]
                * grad_framed[
                    2 - row_shift : 2 - row_shift + tile_rows,
                    2 - col_shift : 2 - col_shift + full_width,
                ]
            )
            short_cols.append(
                jnp.sum(
                    grad_feat
                    * framed[row_shift : row_shift + tile_rows, col_shift : col_shift + full_width],
                    axis=(0, 1),
                )
            )
        short_rows.append(jnp.stack(short_cols))
    back_stack = back_sum.astype(jnp.bfloat16)
    short_term = jnp.stack(short_rows).reshape(3, 3, 2, channels).transpose(2, 0, 1, 3) * scale
    short_grad = taken_together(short_term, "grid")
    weight_term = (
        jnp.einsum("rwd,rwc->dc", gathered, back_stack, preferred_element_type=jnp.float32) * scale
    )
    gate_grad, value_grad, row_share, col_share = (
        *tuple(
            (
                part.astype(jnp.float32)
                for part in in_one_piece(
                    (
                        weight_term[:, :channels].astype(jnp.bfloat16),
                        weight_term[:, channels:].astype(jnp.bfloat16),
                    ),
                    "grid",
                    0,
                    1,
                )
            )
        ),
        lax.psum_scatter(
            row_grad.astype(jnp.bfloat16), "grid", scatter_dimension=0, tiled=True
        ).astype(jnp.float32),
        lax.psum_scatter(
            col_grad.astype(jnp.bfloat16), "grid", scatter_dimension=0, tiled=True
        ).astype(jnp.float32),
    )
    partial_term = jnp.einsum("rwc,dc->rwd", back_stack, w_both, preferred_element_type=jnp.float32)
    input_grad = lax.psum_scatter(
        partial_term.astype(jnp.bfloat16), "ch", scatter_dimension=2, tiled=True
    )
    return (gated, input_grad, gate_grad, value_grad, short_grad, row_share, col_share)


def solution(mesh):
    return jax.shard_map(
        local,
        mesh=mesh,
        in_specs=(
            P("grid", None, "ch"),
            P(None, "ch"),
            P(None, "ch"),
            P(None, None, None, "ch"),
            P(None, "ch"),
            P(None, "ch"),
            P("grid", None, "ch"),
        ),
        out_specs=(
            P("grid", None, "ch"),
            P("grid", None, "ch"),
            P("grid", "ch"),
            P("grid", "ch"),
            P(None, None, None, "ch"),
            P("grid", "ch"),
            P("grid", "ch"),
        ),
        check_vma=False,
    )
```

profile of v0, /device:TPU:1, one launch (start us, length us, event | category | flops | bytes accessed | tf_op | source)
XLA Modules:
  0.0 852.9 jit_solution(1161996941468640835)
XLA Ops:
  8.1 20.8 %fusion.43 = f32[1024,128]{1,0:T(8,128)S(1)} fusion(bf16[1024,128]{1,0:T(8,128)(2,1)S(1)} %copy-done), kind=kOutput, calls=%fused_computation.93 | convolution fusion | flops 1626341376 | bytes 786432 | tf_op jit(solution)/shard_map/mc,mk->kc/dot_general | solution.py:112
  30.1 22.3 %all-gather.2.cloned.1.call-done = bf16[4,1024,512]{2,1,0:T(8,128)(2,1)} async-done(((bf16[4,1024,128]{2,1,0:T(8,128)(2,1)}), bf16[4,1024,512]{2,1,0:T(8,128)(2,1)}) %all-gather.2.cloned.1.call-update) | async-done | bytes 4194320 | tf_op jit(solution)/shard_map/all_gather | solution.py:86
  88.5 17.2 %fusion.26 = f32[1024,4,128]{2,0,1:T(8,128)S(1)} fusion(bf16[4,1024,256]{1,2,0:T(8,128)(2,1)S(1)} %add_convert_fusion), kind=kOutput, calls=%fused_computation.67 | convolution fusion | flops 1093664768 | bytes 3145728 | tf_op jit(solution)/shard_map/rwc,wk->rkc/dot_general | solution.py:109
  105.7 18.4 %add_bitcast_fusion = f32[4,1024,128]{2,1,0:T(8,128)S(1)} fusion(f32[1024,4,128]{2,0,1:T(8,128)S(1)} %fusion.26, bf16[4,1024,256]{1,2,0:T(8,128)(2,1)} %copy-done.11), kind=kOutput, calls=%fused_computation.90 | convolution fusion | flops 1091043328 | bytes 5242880 | tf_op jit(solution)/shard_map/rwc,wk->rkc/dot_general | solution.py:108
  125.7 17.4 %rev.25 = f32[4,1023,128]{2,1,0:T(8,128)} reverse(f32[4,1023,128]{2,1,0:T(8,128)} %slice.247), dimensions={1} | reverse | bytes 4190208 | tf_op jit(solution)/shard_map/jit(_flip)/rev | solution.py:51
  145.1 30.1 %multiply_bitcast_fusion.1 = f32[4,1024,128]{1,2,0:T(8,128)S(1)} fusion(f32[4,1024,128]{2,1,0:T(8,128)S(1)} %fusion.175), kind=kOutput, calls=%fused_computation.86 | convolution fusion | flops 6458703872 | bytes 4194304 | tf_op jit(solution)/shard_map/rkc,kw->rwc/dot_general | solution.py:115
  177.1 8.8 %all-to-all-start = ((f32[4,1024,128]{2,0,1:T(4,128)}), f32[4,1024,128]{2,0,1:T(4,128)S(1)}, u32[]{:S(2)}, u32[]{:S(2)}) async-start(f32[4,1024,128]{2,0,1:T(4,128)} %copy.99), calls=%async_computation | async-start | bytes 4194304 | tf_op jit(solution)/shard_map/all_to_all | solution.py:125
  189.2 22.6 %all-to-all-done = f32[4,1024,128]{2,0,1:T(4,128)S(1)} async-done(((f32[4,1024,128]{2,0,1:T(4,128)}), f32[4,1024,128]{2,0,1:T(4,128)S(1)}, u32[]{:S(2)}, u32[]{:S(2)}) %all-to-all-start) | async-done | bytes 2097184 | tf_op jit(solution)/shard_map/all_to_all | solution.py:125
  217.0 16.6 %rev.27 = f32[127,32,128]{2,0,1:T(8,128)} reverse(f32[127,32,128]{2,0,1:T(8,128)} %slice.251), dimensions={0} | reverse | bytes 4161536 | tf_op jit(solution)/shard_map/jit(_flip)/rev | solution.py:51
  250.8 25.1 %all-to-all-done.1 = f32[128,32,128]{2,1,0:T(8,128)S(1)} async-done(((f32[128,32,128]{2,1,0:T(8,128)}), f32[128,32,128]{2,1,0:T(8,128)S(1)}, u32[]{:S(2)}, u32[]{:S(2)}) %all-to-all-start.1) | async-done | bytes 2097184 | tf_op jit(solution)/shard_map/all_to_all | solution.py:127
  285.9 33.2 %all_to_all.77 = f32[4,1024,128]{2,0,1:T(4,128)S(1)} all-to-all(f32[4,1024,128]{2,0,1:T(4,128)S(1)} %copy.107), channel_id=1, replica_groups=mesh['grid'=32,'ch'=4] {'grid'}, dimensions={1} | all-to-all | bytes 4194304 | tf_op jit(solution)/shard_map/all_to_all | solution.py:128
  324.5 16.6 %rev.28 = f32[127,32,128]{2,0,1:T(8,128)} reverse(f32[127,32,128]{2,0,1:T(8,128)} %slice.253), dimensions={0} | reverse | bytes 4161536 | tf_op jit(solution)/shard_map/jit(_flip)/rev | solution.py:51
  353.0 17.9 %fusion.178 = f32[1024,1024,1]{1,0,2:T(8,128)} fusion(), kind=kLoop, calls=%fused_computation.39.clone.clone.clone.1 | loop fusion | flops 15728640 | bytes 4194304 | tf_op jit(solution)/shard_map/rwc,wk->rkc/dot_general | solution.py:135
  370.9 17.5 %sine_add_fusion.20 = f32[1024,1024]{1,0:T(8,128)} fusion(), kind=kLoop, calls=%fused_computation.52.clone.1.clone.1 | loop fusion | flops 15728640 | bytes 4194304
  399.6 17.1 %rev.29 = f32[4,1023,128]{2,1,0:T(8,128)} reverse(f32[4,1023,128]{2,1,0:T(8,128)} %slice.255), dimensions={1} | reverse | bytes 4190208 | tf_op jit(solution)/shard_map/jit(_flip)/rev | solution.py:51
  424.6 9.1 %fusion.41 = f32[1024,512]{0,1:S(1)} fusion(f32[1024,512]{0,1:T(8,128)S(1)} %bitcast.133, f32[1024,1024]{1,0:T(8,128)} %sine_add_fusion.20), kind=kOutput, calls=%fused_computation.91 | convolution fusion | flops 6442450944 | bytes 8388608
  441.3 25.0 %fusion.64 = bf16[1024,128]{1,0:T(8,128)(2,1)} fusion(f32[1024,128]{1,0:T(8,128)S(1)} %copy-done.14), kind=kOutput, calls=%fused_computation.102 | convolution fusion | flops 1626603520 | bytes 786432 | tf_op jit(solution)/shard_map/kc,km->mc/dot_general | solution.py:141
  466.4 8.7 %select_maximum_fusion = f32[6,1026,256]{1,2,0:T(8,128)} fusion(f32[1,1024,256]{1,2,0:T(8,128)} %collective-permute-done.3, f32[1,1024,256]{1,2,0:T(8,128)S(1)} %collective-permute-done.2, f32[4,1024,128]{1,2,0:T(8,128)S(1)} %multiply_bitcast_fusion, f32[4,1024,128]{1,2,0:T(8,128)} %get-tuple-element.56), kind=kLoop, calls=%fused_computation.2 | loop fusion | flops 15759360 | bytes 12595200 | tf_op jit(solution)/shard_map/concatenate | solution.py:19
  475.1 15.5 %fusion.5 = bf16[4,1024,256]{1,2,0:T(8,128)(2,1)} fusion(f32[6,1026,256]{1,2,0:T(8,128)} %select_maximum_fusion, f32[1,1024,256]{1,2,0:T(8,128)S(1)} %collective-permute-done.2, f32[4,1024,128]{1,2,0:T(8,128)S(1)} %multiply_bitcast_fusion, f32[4,1024,128]{1,2,0:T(8,128)} %get-tuple-element.56, f32[1,1024,256]{1,2,0:T(8,128)} %collective-permute-done.3, ...), kind=kLoop, calls=%fused_computation.19 | loop fusion | flops 24117248 | bytes 33563648 | tf_op jit(solution)/shard_map/convert_element_type | solution.py:168
  523.1 19.8 %multiply_reduce_fusion.7 = (f32[256]{0:T(256)S(1)}, f32[256]{0:T(256)S(1)}, f32[256]{0:T(256)S(1)}, f32[256]{0:T(256)S(1)}, f32[256]{0:T(256)S(1)}, /*index=5*/...) fusion(f32[6,1026,256]{1,2,0:T(8,128)} %copy-done.2, f32[4,1024,128]{1,2,0:T(8,128)S(1)} %multiply_bitcast_fusion, ...), kind=kLoop, calls=%fused_computation.49 | loop fusion | flops 19920640 | bytes 41952256 | tf_op jit(solution)/shard_map/reduce_sum | solution.py:161
  543.8 9.0 %all-to-all-start.4 = ((f32[32,2,3,3,128]{4,1,3,2,0:T(2,128)}), f32[32,2,3,3,128]{4,1,3,2,0:T(2,128)S(1)}, u32[]{:S(2)}, u32[]{:S(2)}) async-start(f32[32,2,3,3,128]{4,1,3,2,0:T(2,128)} %broadcast_in_dim.2), calls=%async_computation.4 | async-start | bytes 589824 | tf_op jit(solution)/shard_map/all_to_all | solution.py:25
  553.3 132.1 %all-reduce.2 = bf16[128,128]{1,0:T(8,128)(2,1)S(1)} all-reduce(bf16[128,128]{1,0:T(8,128)(2,1)S(1)} %fusion.67), channel_id=5, replica_groups=mesh['grid'=32,'ch'=4] {'grid'}, use_global_device_ids=true, to_apply=%region_15.16.clone | all-reduce | flops 16384 | bytes 65536
  687.9 79.1 %reduce-scatter.12.cloned.1.call-done = bf16[16,256]{1,0:T(8,128)(2,1)} async-done(((bf16[512,256]{1,0:T(8,128)(2,1)}), bf16[16,256]{1,0:T(8,128)(2,1)}) %reduce-scatter.12.cloned.1.call-update) | async-done | bytes 8208
  769.4 73.2 %reduce-scatter.10.cloned.1.call-done = bf16[128,4096]{1,0:T(8,128)(2,1)} async-done(((bf16[512,4096]{1,0:T(8,128)(2,1)}), bf16[128,4096]{1,0:T(8,128)(2,1)}) %reduce-scatter.10.cloned.1.call-update) | async-done | bytes 1048592
  (135 shorter events, 164.4 us)
Async XLA Ops:
  7.2 45.2 %all-gather.2.cloned.1.call-start = ((), (), s32[]{:S(2)}) async-start(), calls=%async_computation.8 | async-start | bytes 5242880 | tf_op jit(solution)/shard_map/all_gather | solution.py:86
  8.1 21.7 %copy-start.16 = (bf16[512,128]{1,0:T(8,128)(2,1)S(1)}, bf16[512,128]{1,0:T(8,128)(2,1)}, u32[]{:S(2)}) copy-start(bf16[512,128]{1,0:T(8,128)(2,1)} %param.8) | copy-start | bytes 393220
  8.1 21.8 %copy-start.17 = (bf16[512,128]{1,0:T(8,128)(2,1)S(1)}, bf16[512,128]{1,0:T(8,128)(2,1)}, u32[]{:S(2)}) copy-start(bf16[512,128]{1,0:T(8,128)(2,1)} %param.9) | copy-start | bytes 393220
  30.1 32.1 %copy-start.18 = (bf16[2,3,3,128]{3,0,2,1:T(2,128)(2,1)S(1)}, bf16[2,3,3,128]{3,0,2,1:T(2,128)(2,1)}, u32[]{:S(2)}) copy-start(bf16[2,3,3,128]{3,0,2,1:T(2,128)(2,1)} %param.10) | copy-start | bytes 13828
  30.1 34.9 %slice-start = ((f32[1024,128]{1,0:T(8,128)}), f32[1,128]{1,0:T(1,128)S(1)}, s32[]{:S(2)}) async-start(f32[1024,128]{1,0:T(8,128)} %copy-done.13), calls=%async_computation.12 | async-start | bytes 1024 | tf_op jit(solution)/shard_map/slice | solution.py:49
  56.9 14.5 %collective-permute-start = (bf16[1,1024,256]{1,2,0:T(8,128)(2,1)}, bf16[1,1024,256]{1,2,0:T(8,128)(2,1)}, u32[]{:S(2)}, u32[]{:S(2)}) collective-permute-start(bf16[1,1024,256]{1,2,0:T(8,128)(2,1)} %get-tuple-element.57), channel_id=1, source_target_pairs={{0,4},{4,8},{8,12},{12,16},{16,20},{20,24},{24,28},{28,32},{32,36}... | collective-permute-start | bytes 1572872 | tf_op jit(solution)/shard_map/ppermute | solution.py:17
  60.9 15.1 %collective-permute-start.1 = (bf16[1,1024,256]{1,2,0:T(8,128)(2,1)}, bf16[1,1024,256]{1,2,0:T(8,128)(2,1)}, u32[]{:S(2)}, u32[]{:S(2)}) collective-permute-start(bf16[1,1024,256]{1,2,0:T(8,128)(2,1)} %get-tuple-element.58), channel_id=1, source_target_pairs={{4,0},{8,4},{12,8},{16,12},{20,16},{24,20},{28,24},{32,28},{36,32}... | collective-permute-start | bytes 1572872 | tf_op jit(solution)/shard_map/ppermute | solution.py:18
  79.2 7.9 copy-start.2
  124.1 19.1 %copy-start.7 = (f32[4,1024,128]{2,1,0:T(8,128)}, f32[4,1024,128]{2,1,0:T(8,128)S(1)}, u32[]{:S(2)}) copy-start(f32[4,1024,128]{2,1,0:T(8,128)S(1)} %add_bitcast_fusion) | copy-start | bytes 6291460
  175.2 10.7 %copy-start.19 = (bf16[128,128]{1,0:T(8,128)(2,1)S(1)}, bf16[128,128]{1,0:T(8,128)(2,1)}, u32[]{:S(2)}) copy-start(bf16[128,128]{1,0:T(8,128)(2,1)} %param.12) | copy-start | bytes 98308
  177.1 34.6 %all-to-all-start = ((f32[4,1024,128]{2,0,1:T(4,128)}), f32[4,1024,128]{2,0,1:T(4,128)S(1)}, u32[]{:S(2)}, u32[]{:S(2)}) async-start(f32[4,1024,128]{2,0,1:T(4,128)} %copy.99), calls=%async_computation | async-start | bytes 4194304 | tf_op jit(solution)/shard_map/all_to_all | solution.py:125
  215.4 18.2 %copy-start.5 = (f32[128,32,128]{2,0,1:T(8,128)}, f32[128,32,128]{2,0,1:T(8,128)S(1)}, u32[]{:S(2)}) copy-start(f32[128,32,128]{2,0,1:T(8,128)S(1)} %fusion.85) | copy-start | bytes 6291460
  240.2 35.7 %all-to-all-start.1 = ((f32[128,32,128]{2,1,0:T(8,128)}), f32[128,32,128]{2,1,0:T(8,128)S(1)}, u32[]{:S(2)}, u32[]{:S(2)}) async-start(f32[128,32,128]{2,1,0:T(8,128)} %copy.102), calls=%async_computation.1 | async-start | bytes 4194304 | tf_op jit(solution)/shard_map/all_to_all | solution.py:127
  322.8 18.2 %copy-start.6 = (f32[128,32,128]{2,0,1:T(8,128)}, f32[128,32,128]{2,0,1:T(8,128)S(1)}, u32[]{:S(2)}) copy-start(f32[128,32,128]{2,0,1:T(8,128)S(1)} %fusion.82) | copy-start | bytes 6291460
  347.7 40.8 %all-to-all-start.3 = ((f32[128,32,128]{2,1,0:T(8,128)}), f32[128,32,128]{2,1,0:T(8,128)S(1)}, u32[]{:S(2)}, u32[]{:S(2)}) async-start(f32[128,32,128]{2,1,0:T(8,128)} %copy.110), calls=%async_computation.3 | async-start | bytes 4194304 | tf_op jit(solution)/shard_map/all_to_all | solution.py:132
  352.9 333.7 %reduce-scatter.8.cloned.1.call-start = ((), (), s32[]{:S(2)}) async-start(), calls=%async_computation.9 | async-start | bytes 270336 | tf_op jit(solution)/shard_map/reduce_scatter | solution.py:189
  397.4 19.2 %copy-start.8 = (f32[4,1024,128]{2,1,0:T(8,128)S(1)}, f32[4,1024,128]{2,1,0:T(8,128)}, u32[]{:S(2)}) copy-start(f32[4,1024,128]{2,1,0:T(8,128)} %copy-done.7) | copy-start | bytes 6291460
  433.9 7.4 copy-start.14
  436.8 29.6 %collective-permute-start.2 = (f32[1,1024,256]{1,2,0:T(8,128)}, f32[1,1024,256]{1,2,0:T(8,128)S(1)}, u32[]{:S(2)}, u32[]{:S(2)}) collective-permute-start(f32[1,1024,256]{1,2,0:T(8,128)} %get-tuple-element.52), channel_id=1, source_target_pairs={{0,4},{4,8},{8,12},{12,16},{16,20},{20,24},{24,28},{28,32},{32,36}... | collective-permute-start | bytes 3145736 | tf_op jit(solution)/shard_map/ppermute | solution.py:17
  440.0 26.4 %collective-permute-start.3 = (f32[1,1024,256]{1,2,0:T(8,128)}, f32[1,1024,256]{1,2,0:T(8,128)}, u32[]{:S(2)}, u32[]{:S(2)}) collective-permute-start(f32[1,1024,256]{1,2,0:T(8,128)} %get-tuple-element.53), channel_id=1, source_target_pairs={{4,0},{8,4},{12,8},{16,12},{20,16},{24,20},{28,24},{32,28},{36,32}... | collective-permute-start | bytes 3145736 | tf_op jit(solution)/shard_map/ppermute | solution.py:18
  466.3 300.7 %reduce-scatter.12.cloned.1.call-start = ((), (), s32[]{:S(2)}) async-start(), calls=%async_computation.11 | async-start | bytes 270336
  495.6 347.0 %reduce-scatter.10.cloned.1.call-start = ((), (), s32[]{:S(2)}) async-start(), calls=%async_computation.10 | async-start | bytes 5242880
  523.1 323.0 %copy-start.1 = (bf16[1024,128]{1,0:T(8,128)(2,1)S(1)}, bf16[1024,128]{1,0:T(8,128)(2,1)}, u32[]{:S(2)}) copy-start(bf16[1024,128]{1,0:T(8,128)(2,1)} %param.11) | copy-start | bytes 786436
  543.8 142.2 %all-to-all-start.4 = ((f32[32,2,3,3,128]{4,1,3,2,0:T(2,128)}), f32[32,2,3,3,128]{4,1,3,2,0:T(2,128)S(1)}, u32[]{:S(2)}, u32[]{:S(2)}) async-start(f32[32,2,3,3,128]{4,1,3,2,0:T(2,128)} %broadcast_in_dim.2), calls=%async_computation.4 | async-start | bytes 589824 | tf_op jit(solution)/shard_map/all_to_all | solution.py:25
  (10 other events, 16.7 us)
Sparse Core Ops, SparseCore 0:
  9.7 42.6 all-gather.1
  466.4 140.0 reduce-scatter.7
  608.9 158.1 reduce-scatter.11
  769.5 72.9 reduce-scatter.9
where the time goes:
time: 865 us; the launch traced here: 853 us
  waiting for transfers between devices  233 us (27%)
  blocking collectives  165 us (19%)
  matrix products  153 us (18%)
  local copies, waits for them, and re-layouts  130 us (15%)
  other arithmetic  115 us (13%)
  starting transfers between devices  41.3 us (5%)
  between operations  15.3 us (2%)
    unnamed x6, waiting for transfers between devices  153 us
    unnamed x1, blocking collectives  132 us
    rev x6, local copies, waits for them, and re-layouts, mirror(): return jnp.concatenate([leading, jnp.flip(remainder, along)], axis=along)  71.1 us
    all_to_all x1, blocking collectives, local(): lax.all_to_all(grad_mix, 'grid', split_axis=1, concat_axis=0, tiled=True)  33.2 us
    unnamed x58, local copies, waits for them, and re-layouts  32.9 us
    dot_general x1, matrix products, local(): jnp.einsum('rkc,kw->rwc', row_mixed, cas_width, precision=highest)  30.1 us
    all_to_all x1, waiting for transfers between devices, local(): lax.all_to_all(mixed_cols, 'grid', split_axis=0, concat_axis=1, tiled=True)  25.1 us
    dot_general x1, matrix products, local(): jnp.einsum('kc,km->mc', row_term, cas_width, precision=highest)  25 us
  transfers between devices with their start and end apart: 12, of which 7 were waited for; matrix products, arithmetic and copies ran while one was open for 20% of the time, Pallas kernels for 0%

commit v1 on v0

--- a/solution.py
+++ b/solution.py
@@ -5,6 +5,11 @@
 from jax.sharding import PartitionSpec as P
 
 highest = lax.Precision.HIGHEST
+
+
+def exchange_gather(x, mesh_axis, dim):
+    sent = jnp.stack([x] * lax.axis_size(mesh_axis))
+    return jnp.concatenate(lax.all_to_all(sent, mesh_axis, 0, 0), axis=dim)
 
 
 def extended(value, sides, width):
@@ -83,7 +88,7 @@
 
 def local(inputs, w_gate, w_value, short_filter, row_filter, column_filter, cotangent):
     tile_rows, full_width, channels = inputs.shape
-    gathered = lax.all_gather(inputs, "ch", axis=2, tiled=True)
+    gathered = exchange_gather(inputs, "ch", 2)
     w_both = jnp.concatenate([w_gate, w_value], axis=1)
     stacked = jnp.einsum(
         "rwd,dc->rwc", gathered, w_both, preferred_element_type=jnp.float32

time: 865 us -> 880 us (1.017)
    all_to_all x0 -> x1, waiting for transfers between devices: none -> 26.8 us  [exchange_gather(): return jnp.concatenate(lax.all_to_all(sent, mesh_axis, 0, 0), axis=dim)]
    all_gather x1 -> x0, waiting for transfers between devices: 22.3 us -> none  [local(): gathered = lax.all_gather(inputs, 'ch', axis=2, tiled=True)]
    unnamed x6 -> x5, waiting for transfers between devices: 153 us -> 152 us
    unnamed x58 -> x100, local copies, waits for them, and re-layouts: 32.9 us -> 32.7 us
where the time goes in v1:
time: 880 us; the launch traced here: 868 us
  waiting for transfers between devices  235 us (27%)
  blocking collectives  168 us (19%)
  matrix products  153 us (17%)
  local copies, waits for them, and re-layouts  135 us (15%)
  other arithmetic  114 us (13%)
  starting transfers between devices  47.8 us (5%)
  between operations  15.5 us (2%)
    unnamed x5, waiting for transfers between devices  152 us
    unnamed x1, blocking collectives  133 us
    rev x6, local copies, waits for them, and re-layouts, mirror(): return jnp.concatenate([leading, jnp.flip(remainder, along)], axis=along)  71.1 us
    all_to_all x1, blocking collectives, local(): lax.all_to_all(grad_mix, 'grid', split_axis=1, concat_axis=0, tiled=True)  34.9 us
    unnamed x100, local copies, waits for them, and re-layouts  32.7 us
    dot_general x1, matrix products, local(): jnp.einsum('rkc,kw->rwc', row_mixed, cas_width, precision=highest)  30.1 us
    all_to_all x1, waiting for transfers between devices, exchange_gather(): return jnp.concatenate(lax.all_to_all(sent, mesh_axis, 0, 0), axis=dim)  26.8 us
    dot_general x1, matrix products, local(): jnp.einsum('kc,km->mc', row_term, cas_width, precision=highest)  25 us
  transfers between devices with their start and end apart: 12, of which 7 were waited for; matrix products, arithmetic and copies ran while one was open for 20% of the time, Pallas kernels for 0%

profile of v1, /device:TPU:1, one launch (start us, length us, event | category | flops | bytes accessed | tf_op | source)
XLA Modules:
  0.0 867.6 jit_solution(16025284194241572262)
XLA Ops:
  17.5 20.9 %fusion.49 = f32[1024,128]{1,0:T(8,128)S(1)} fusion(bf16[1024,128]{1,0:T(8,128)(2,1)S(1)} %copy-done), kind=kOutput, calls=%fused_computation.99 | convolution fusion | flops 1626341376 | bytes 786432 | tf_op jit(solution)/shard_map/mc,mk->kc/dot_general | solution.py:117
  39.5 26.8 %all-to-all-done = bf16[4,4,1024,128]{3,2,1,0:T(8,128)(2,1)} async-done(((bf16[4,4,1024,128]{3,2,1,0:T(8,128)(2,1)}), bf16[4,4,1024,128]{3,2,1,0:T(8,128)(2,1)}, u32[]{:S(2)}, u32[]{:S(2)}) %all-to-all-start) | async-done | bytes 4194336 | tf_op jit(solution)/shard_map/all_to_all | solution.py:12
  102.3 17.2 %fusion.32 = f32[1024,4,128]{2,0,1:T(8,128)S(1)} fusion(bf16[4,1024,256]{1,2,0:T(8,128)(2,1)S(1)} %add_convert_fusion), kind=kOutput, calls=%fused_computation.73 | convolution fusion | flops 1093664768 | bytes 3145728 | tf_op jit(solution)/shard_map/rwc,wk->rkc/dot_general | solution.py:114
  119.4 18.4 %add_bitcast_fusion = f32[4,1024,128]{2,1,0:T(8,128)S(1)} fusion(f32[1024,4,128]{2,0,1:T(8,128)S(1)} %fusion.32, bf16[4,1024,256]{1,2,0:T(8,128)(2,1)} %copy-done.11), kind=kOutput, calls=%fused_computation.96 | convolution fusion | flops 1091043328 | bytes 5242880 | tf_op jit(solution)/shard_map/rwc,wk->rkc/dot_general | solution.py:113
  139.4 17.4 %rev.25 = f32[4,1023,128]{2,1,0:T(8,128)} reverse(f32[4,1023,128]{2,1,0:T(8,128)} %slice.247), dimensions={1} | reverse | bytes 4190208 | tf_op jit(solution)/shard_map/jit(_flip)/rev | solution.py:56
  158.7 30.1 %multiply_bitcast_fusion.1 = f32[4,1024,128]{1,2,0:T(8,128)S(1)} fusion(f32[4,1024,128]{2,1,0:T(8,128)S(1)} %fusion.192), kind=kOutput, calls=%fused_computation.92 | convolution fusion | flops 6458703872 | bytes 4194304 | tf_op jit(solution)/shard_map/rkc,kw->rwc/dot_general | solution.py:120
  190.7 9.8 %all-to-all-start.1 = ((f32[4,1024,128]{2,0,1:T(4,128)}), f32[4,1024,128]{2,0,1:T(4,128)S(1)}, u32[]{:S(2)}, u32[]{:S(2)}) async-start(f32[4,1024,128]{2,0,1:T(4,128)} %copy.101), calls=%async_computation.1 | async-start | bytes 4194304 | tf_op jit(solution)/shard_map/all_to_all | solution.py:130
  203.1 23.8 %all-to-all-done.1 = f32[4,1024,128]{2,0,1:T(4,128)S(1)} async-done(((f32[4,1024,128]{2,0,1:T(4,128)}), f32[4,1024,128]{2,0,1:T(4,128)S(1)}, u32[]{:S(2)}, u32[]{:S(2)}) %all-to-all-start.1) | async-done | bytes 2097184 | tf_op jit(solution)/shard_map/all_to_all | solution.py:130
  232.2 16.6 %rev.27 = f32[127,32,128]{2,0,1:T(8,128)} reverse(f32[127,32,128]{2,0,1:T(8,128)} %slice.251), dimensions={0} | reverse | bytes 4161536 | tf_op jit(solution)/shard_map/jit(_flip)/rev | solution.py:56
  264.8 23.2 %all-to-all-done.2 = f32[128,32,128]{2,1,0:T(8,128)S(1)} async-done(((f32[128,32,128]{2,1,0:T(8,128)}), f32[128,32,128]{2,1,0:T(8,128)S(1)}, u32[]{:S(2)}, u32[]{:S(2)}) %all-to-all-start.2) | async-done | bytes 2097184 | tf_op jit(solution)/shard_map/all_to_all | solution.py:132
  298.0 34.9 %all_to_all.82 = f32[4,1024,128]{2,0,1:T(4,128)S(1)} all-to-all(f32[4,1024,128]{2,0,1:T(4,128)S(1)} %copy.109), channel_id=1, replica_groups=mesh['grid'=32,'ch'=4] {'grid'}, dimensions={1} | all-to-all | bytes 4194304 | tf_op jit(solution)/shard_map/all_to_all | solution.py:133
  338.8 16.6 %rev.28 = f32[127,32,128]{2,0,1:T(8,128)} reverse(f32[127,32,128]{2,0,1:T(8,128)} %slice.253), dimensions={0} | reverse | bytes 4161536 | tf_op jit(solution)/shard_map/jit(_flip)/rev | solution.py:56
  367.4 17.9 %fusion.195 = f32[1024,1024,1]{1,0,2:T(8,128)} fusion(), kind=kLoop, calls=%fused_computation.43.clone.clone.clone.1 | loop fusion | flops 15728640 | bytes 4194304 | tf_op jit(solution)/shard_map/rwc,wk->rkc/dot_general | solution.py:140
  385.4 17.5 %sine_add_fusion.20 = f32[1024,1024]{1,0:T(8,128)} fusion(), kind=kLoop, calls=%fused_computation.56.clone.1.clone.1 | loop fusion | flops 15728640 | bytes 4194304
  414.0 17.1 %rev.29 = f32[4,1023,128]{2,1,0:T(8,128)} reverse(f32[4,1023,128]{2,1,0:T(8,128)} %slice.255), dimensions={1} | reverse | bytes 4190208 | tf_op jit(solution)/shard_map/jit(_flip)/rev | solution.py:56
  439.0 9.1 %fusion.47 = f32[1024,512]{0,1:S(1)} fusion(f32[1024,512]{0,1:T(8,128)S(1)} %bitcast.154, f32[1024,1024]{1,0:T(8,128)} %sine_add_fusion.20), kind=kOutput, calls=%fused_computation.97 | convolution fusion | flops 6442450944 | bytes 8388608
  455.7 25.0 %fusion.77 = bf16[1024,128]{1,0:T(8,128)(2,1)} fusion(f32[1024,128]{1,0:T(8,128)S(1)} %copy-done.14), kind=kOutput, calls=%fused_computation.108 | convolution fusion | flops 1626603520 | bytes 786432 | tf_op jit(solution)/shard_map/kc,km->mc/dot_general | solution.py:146
  480.9 8.9 %select_maximum_fusion = f32[6,1026,256]{1,2,0:T(8,128)} fusion(f32[1,1024,256]{1,2,0:T(8,128)} %collective-permute-done.3, f32[1,1024,256]{1,2,0:T(8,128)S(1)} %collective-permute-done.2, f32[4,1024,128]{1,2,0:T(8,128)S(1)} %multiply_bitcast_fusion, f32[4,1024,128]{1,2,0:T(8,128)} %get-tuple-element.56), kind=kLoop, calls=%fused_computation.2 | loop fusion | flops 15759360 | bytes 12595200 | tf_op jit(solution)/shard_map/concatenate | solution.py:24
  489.8 15.1 %fusion.9 = bf16[4,1024,256]{1,2,0:T(8,128)(2,1)} fusion(f32[6,1026,256]{1,2,0:T(8,128)} %select_maximum_fusion, f32[1,1024,256]{1,2,0:T(8,128)S(1)} %collective-permute-done.2, f32[4,1024,128]{1,2,0:T(8,128)S(1)} %multiply_bitcast_fusion, f32[4,1024,128]{1,2,0:T(8,128)} %get-tuple-element.56, f32[1,1024,256]{1,2,0:T(8,128)} %collective-permute-done.3, ...), kind=kLoop, calls=%fused_computation.23 | loop fusion | flops 24117248 | bytes 33563648 | tf_op jit(solution)/shard_map/convert_element_type | solution.py:173
  537.3 19.9 %multiply_reduce_fusion.7 = (f32[256]{0:T(256)S(1)}, f32[256]{0:T(256)S(1)}, f32[256]{0:T(256)S(1)}, f32[256]{0:T(256)S(1)}, f32[256]{0:T(256)S(1)}, /*index=5*/...) fusion(f32[6,1026,256]{1,2,0:T(8,128)} %copy-done.2, f32[4,1024,128]{1,2,0:T(8,128)S(1)} %multiply_bitcast_fusion, ...), kind=kLoop, calls=%fused_computation.53 | loop fusion | flops 19920640 | bytes 41952256 | tf_op jit(solution)/shard_map/reduce_sum | solution.py:166
  558.0 9.0 %all-to-all-start.5 = ((f32[32,2,3,3,128]{4,1,3,2,0:T(2,128)}), f32[32,2,3,3,128]{4,1,3,2,0:T(2,128)S(1)}, u32[]{:S(2)}, u32[]{:S(2)}) async-start(f32[32,2,3,3,128]{4,1,3,2,0:T(2,128)} %broadcast_in_dim.2), calls=%async_computation.5 | async-start | bytes 589824 | tf_op jit(solution)/shard_map/all_to_all | solution.py:30
  567.5 132.9 %all-reduce.2 = bf16[128,128]{1,0:T(8,128)(2,1)S(1)} all-reduce(bf16[128,128]{1,0:T(8,128)(2,1)S(1)} %fusion.84), channel_id=5, replica_groups=mesh['grid'=32,'ch'=4] {'grid'}, use_global_device_ids=true, to_apply=%region_15.16.clone | all-reduce | flops 16384 | bytes 65536
  703.0 78.6 %reduce-scatter.12.cloned.1.call-done = bf16[16,256]{1,0:T(8,128)(2,1)} async-done(((bf16[512,256]{1,0:T(8,128)(2,1)}), bf16[16,256]{1,0:T(8,128)(2,1)}) %reduce-scatter.12.cloned.1.call-update) | async-done | bytes 8208
  783.9 73.3 %reduce-scatter.10.cloned.1.call-done = bf16[128,4096]{1,0:T(8,128)(2,1)} async-done(((bf16[512,4096]{1,0:T(8,128)(2,1)}), bf16[128,4096]{1,0:T(8,128)(2,1)}) %reduce-scatter.10.cloned.1.call-update) | async-done | bytes 1048592
  (177 shorter events, 172.2 us)
Async XLA Ops:
  11.3 55.0 %all-to-all-start = ((bf16[4,4,1024,128]{3,2,1,0:T(8,128)(2,1)}), bf16[4,4,1024,128]{3,2,1,0:T(8,128)(2,1)}, u32[]{:S(2)}, u32[]{:S(2)}) async-start(bf16[4,4,1024,128]{3,2,1,0:T(8,128)(2,1)} %stack.49), calls=%async_computation | async-start | bytes 8388608 | tf_op jit(solution)/shard_map/all_to_all | solution.py:12
  17.5 21.7 %copy-start.17 = (bf16[512,128]{1,0:T(8,128)(2,1)S(1)}, bf16[512,128]{1,0:T(8,128)(2,1)}, u32[]{:S(2)}) copy-start(bf16[512,128]{1,0:T(8,128)(2,1)} %param.8) | copy-start | bytes 393220
  17.5 21.8 %copy-start.18 = (bf16[512,128]{1,0:T(8,128)(2,1)S(1)}, bf16[512,128]{1,0:T(8,128)(2,1)}, u32[]{:S(2)}) copy-start(bf16[512,128]{1,0:T(8,128)(2,1)} %param.9) | copy-start | bytes 393220
  39.5 37.1 %copy-start.19 = (bf16[2,3,3,128]{3,0,2,1:T(2,128)(2,1)S(1)}, bf16[2,3,3,128]{3,0,2,1:T(2,128)(2,1)}, u32[]{:S(2)}) copy-start(bf16[2,3,3,128]{3,0,2,1:T(2,128)(2,1)} %param.10) | copy-start | bytes 13828
  39.5 39.9 %slice-start = ((f32[1024,128]{1,0:T(8,128)}), f32[1,128]{1,0:T(1,128)S(1)}, s32[]{:S(2)}) async-start(f32[1024,128]{1,0:T(8,128)} %copy-done.13), calls=%async_computation.12 | async-start | bytes 1024 | tf_op jit(solution)/shard_map/slice | solution.py:54
  70.8 14.2 %collective-permute-start = (bf16[1,1024,256]{1,2,0:T(8,128)(2,1)}, bf16[1,1024,256]{1,2,0:T(8,128)(2,1)}, u32[]{:S(2)}, u32[]{:S(2)}) collective-permute-start(bf16[1,1024,256]{1,2,0:T(8,128)(2,1)} %get-tuple-element.57), channel_id=1, source_target_pairs={{0,4},{4,8},{8,12},{12,16},{16,20},{20,24},{24,28},{28,32},{32,36}... | collective-permute-start | bytes 1572872 | tf_op jit(solution)/shard_map/ppermute | solution.py:22
  75.3 14.4 %collective-permute-start.1 = (bf16[1,1024,256]{1,2,0:T(8,128)(2,1)}, bf16[1,1024,256]{1,2,0:T(8,128)(2,1)}, u32[]{:S(2)}, u32[]{:S(2)}) collective-permute-start(bf16[1,1024,256]{1,2,0:T(8,128)(2,1)} %get-tuple-element.58), channel_id=1, source_target_pairs={{4,0},{8,4},{12,8},{16,12},{20,16},{24,20},{28,24},{32,28},{36,32}... | collective-permute-start | bytes 1572872 | tf_op jit(solution)/shard_map/ppermute | solution.py:23
  79.4 13.6 %copy-start.22 = (f32[1,1,256]{2,1,0:T(1,128)}, f32[1,1,256]{2,1,0:T(1,128)S(1)}, u32[]{:S(2)}) copy-start(f32[1,1,256]{2,1,0:T(1,128)S(1)} %get-tuple-element.65) | copy-start | bytes 3076
  137.8 19.0 %copy-start.7 = (f32[4,1024,128]{2,1,0:T(8,128)}, f32[4,1024,128]{2,1,0:T(8,128)S(1)}, u32[]{:S(2)}) copy-start(f32[4,1024,128]{2,1,0:T(8,128)S(1)} %add_bitcast_fusion) | copy-start | bytes 6291460
  139.4 19.4 %copy-start.20 = (f32[4,1,128]{2,1,0:T(1,128)}, f32[4,1,128]{2,1,0:T(1,128)S(1)}, u32[]{:S(2)}) copy-start(f32[4,1,128]{2,1,0:T(1,128)S(1)} %slice.246) | copy-start | bytes 6148
  190.7 36.2 %all-to-all-start.1 = ((f32[4,1024,128]{2,0,1:T(4,128)}), f32[4,1024,128]{2,0,1:T(4,128)S(1)}, u32[]{:S(2)}, u32[]{:S(2)}) async-start(f32[4,1024,128]{2,0,1:T(4,128)} %copy.101), calls=%async_computation.1 | async-start | bytes 4194304 | tf_op jit(solution)/shard_map/all_to_all | solution.py:130
  230.6 18.3 %copy-start.5 = (f32[128,32,128]{2,0,1:T(8,128)}, f32[128,32,128]{2,0,1:T(8,128)S(1)}, u32[]{:S(2)}) copy-start(f32[128,32,128]{2,0,1:T(8,128)S(1)} %fusion.102) | copy-start | bytes 6291460
  255.4 32.6 %all-to-all-start.2 = ((f32[128,32,128]{2,1,0:T(8,128)}), f32[128,32,128]{2,1,0:T(8,128)S(1)}, u32[]{:S(2)}, u32[]{:S(2)}) async-start(f32[128,32,128]{2,1,0:T(8,128)} %copy.104), calls=%async_computation.2 | async-start | bytes 4194304 | tf_op jit(solution)/shard_map/all_to_all | solution.py:132
  336.6 18.9 %copy-start.6 = (f32[128,32,128]{2,0,1:T(8,128)}, f32[128,32,128]{2,0,1:T(8,128)S(1)}, u32[]{:S(2)}) copy-start(f32[128,32,128]{2,0,1:T(8,128)S(1)} %fusion.99) | copy-start | bytes 6291460
  362.0 40.9 %all-to-all-start.4 = ((f32[128,32,128]{2,1,0:T(8,128)}), f32[128,32,128]{2,1,0:T(8,128)S(1)}, u32[]{:S(2)}, u32[]{:S(2)}) async-start(f32[128,32,128]{2,1,0:T(8,128)} %copy.112), calls=%async_computation.4 | async-start | bytes 4194304 | tf_op jit(solution)/shard_map/all_to_all | solution.py:137
  367.4 334.3 %reduce-scatter.8.cloned.1.call-start = ((), (), s32[]{:S(2)}) async-start(), calls=%async_computation.9 | async-start | bytes 270336 | tf_op jit(solution)/shard_map/reduce_scatter | solution.py:194
  411.9 19.2 %copy-start.8 = (f32[4,1024,128]{2,1,0:T(8,128)S(1)}, f32[4,1024,128]{2,1,0:T(8,128)}, u32[]{:S(2)}) copy-start(f32[4,1024,128]{2,1,0:T(8,128)} %copy-done.7) | copy-start | bytes 6291460
  411.9 19.2 %copy-start.21 = (f32[4,1,128]{2,1,0:T(1,128)S(1)}, f32[4,1,128]{2,1,0:T(1,128)}, u32[]{:S(2)}) copy-start(f32[4,1,128]{2,1,0:T(1,128)} %copy-done.20) | copy-start | bytes 6148
  451.2 29.7 %collective-permute-start.2 = (f32[1,1024,256]{1,2,0:T(8,128)}, f32[1,1024,256]{1,2,0:T(8,128)S(1)}, u32[]{:S(2)}, u32[]{:S(2)}) collective-permute-start(f32[1,1024,256]{1,2,0:T(8,128)} %get-tuple-element.52), channel_id=1, source_target_pairs={{0,4},{4,8},{8,12},{12,16},{16,20},{20,24},{24,28},{28,32},{32,36}... | collective-permute-start | bytes 3145736 | tf_op jit(solution)/shard_map/ppermute | solution.py:22
  454.4 26.5 %collective-permute-start.3 = (f32[1,1024,256]{1,2,0:T(8,128)}, f32[1,1024,256]{1,2,0:T(8,128)}, u32[]{:S(2)}, u32[]{:S(2)}) collective-permute-start(f32[1,1024,256]{1,2,0:T(8,128)} %get-tuple-element.53), channel_id=1, source_target_pairs={{4,0},{8,4},{12,8},{16,12},{20,16},{24,20},{28,24},{32,28},{36,32}... | collective-permute-start | bytes 3145736 | tf_op jit(solution)/shard_map/ppermute | solution.py:23
  480.8 300.8 %reduce-scatter.12.cloned.1.call-start = ((), (), s32[]{:S(2)}) async-start(), calls=%async_computation.11 | async-start | bytes 270336
  509.8 347.4 %reduce-scatter.10.cloned.1.call-start = ((), (), s32[]{:S(2)}) async-start(), calls=%async_computation.10 | async-start | bytes 5242880
  537.3 323.4 %copy-start.1 = (bf16[1024,128]{1,0:T(8,128)(2,1)S(1)}, bf16[1024,128]{1,0:T(8,128)(2,1)}, u32[]{:S(2)}) copy-start(bf16[1024,128]{1,0:T(8,128)(2,1)} %param.11) | copy-start | bytes 786436
  558.0 143.0 %all-to-all-start.5 = ((f32[32,2,3,3,128]{4,1,3,2,0:T(2,128)}), f32[32,2,3,3,128]{4,1,3,2,0:T(2,128)S(1)}, u32[]{:S(2)}, u32[]{:S(2)}) async-start(f32[32,2,3,3,128]{4,1,3,2,0:T(2,128)} %broadcast_in_dim.2), calls=%async_computation.5 | async-start | bytes 589824 | tf_op jit(solution)/shard_map/all_to_all | solution.py:30
  (31 other events, 246.2 us)
Sparse Core Ops, SparseCore 0:
  480.8 140.2 reduce-scatter.7
  623.5 158.0 reduce-scatter.11
  784.3 72.8 reduce-scatter.9
